TPU v7x, 256 devices: a whole 4x4x8 slice. The times are simulated.
256 devices in a mesh: seq: 32 (over x, y, core), head: 8 (over z).
Axes of the slice: x: 4, y: 4, z: 8, core: 2. Of those that a mesh axis runs over, the one named last changes fastest.
Arguments:
- queries: float32 [16384, 1024], P('seq', 'head'), may hold values from -6 to 6
- keys: float32 [16384, 1024], P('seq', 'head'), may hold values from -5 to 5
- values: float32 [16384, 1024], P('seq', 'head'), may hold values from -15 to 15
- gain: float32 [1024], P('head'), may hold values from 0.1 to 1.9
- ridge: float32 [8], P('head'), may hold values from 0.01 to 0.1
- prior_gram: float32 [8, 128, 128], P('head'), as said below
- prior_cross: float32 [8, 128, 128], P('head')
- cotangent: float32 [16384, 1024], P('seq', 'head'), may hold values from -6 to 6
Outputs:
- normed: float32 [16384, 1024], P('seq', 'head')
- grad_queries: float32 [16384, 1024], P('seq', 'head')
- grad_keys: float32 [16384, 1024], P('seq', 'head')
- grad_values: float32 [16384, 1024], P('seq', 'head')
Inputs may be any that keep to these rules, and one draw needn't show every extreme that they name: `prior_gram`: each head's matrix is symmetric positive definite.
All inputs are finite; a program needn't handle non-finite values.
Results may differ from a plain program's by a relative error of at most 0.0003.
Values sent between devices are 32-bit elements; how exact they have to be, the bound alone decides.
A program may use at most 64 MiB of HBM per device.

v0:
```python
import jax
import jax.numpy as jnp
from jax import lax
from jax.sharding import PartitionSpec as P

DH = 128
ITERS = 8


epsilon = 1e-06


def prefix(part, axis, combine, identity, reverse):
    count = lax.axis_size(axis)
    place = lax.axis_index(axis)
    ahead = count - 1 - place if reverse else place
    gathered = jax.tree.map(lambda a: lax.all_gather(a, axis), part)
    state = jax.tree.map(lambda a, e: jnp.zeros_like(a) + jnp.asarray(e, a.dtype), part, identity)

    def one(turn, state):
        source = count - 1 - turn if reverse else turn
        return combine(
            state, jax.tree.map(lambda a: lax.dynamic_index_in_dim(a, source, 0, False), gathered)
        )

    return lax.fori_loop(0, ahead, one, state)


def block_forward(query, keyset, valueset, start_gram, start_cross, ridge_value, first_row):
    highest = lax.Precision.HIGHEST
    count = query.shape[0]
    places = jnp.arange(count)
    causal = (places[None, :] <= places[:, None]).astype(jnp.float32)
    damping = ridge_value * (first_row + places + 1).astype(jnp.float32)[:, None]

    def apply_system(search):
        inner = jnp.dot(search, keyset.T, precision=highest) * causal
        return (
            jnp.dot(search, start_gram, precision=highest)
            + jnp.dot(inner, keyset, precision=highest)
            + damping * search
        )

    def cg_step(carry, unused):
        solution, residual, search, squared = carry
        image = apply_system(search)
        alpha = squared / jnp.sum(search * image, axis=1, keepdims=True)
        solution = solution + alpha * search
        residual = residual - alpha * image
        squared_next = jnp.sum(residual * residual, axis=1, keepdims=True)
        search = residual + squared_next / squared * search
        return ((solution, residual, search, squared_next), None)

    squared = jnp.sum(query * query, axis=1, keepdims=True)
    start = (jnp.zeros_like(query), query, query, squared)
    (solution, _, _, _), _ = lax.scan(cg_step, start, None, length=ITERS)
    inner = jnp.dot(solution, keyset.T, precision=highest) * causal
    return jnp.dot(solution, start_cross, precision=highest) + jnp.dot(
        inner, valueset, precision=highest
    )


def add_pair(earlier, later):
    return (earlier[0] + later[0], earlier[1] + later[1])


def local(queries, keys, values, gain, ridge, prior_gram, prior_cross, cotangent):
    highest = lax.Precision.HIGHEST
    row_count, width = queries.shape
    heads_here = width // DH

    def split_heads(array):
        return array.reshape(row_count, heads_here, DH).transpose(1, 0, 2)

    def join_heads(array):
        return array.transpose(1, 0, 2).reshape(row_count, width)

    head_q = split_heads(queries)
    head_k = split_heads(keys)
    head_v = split_heads(values)
    own_gram = jnp.einsum("hti,htj->hij", head_k, head_k, precision=highest)
    own_cross = jnp.einsum("hti,htj->hij", head_k, head_v, precision=highest)
    position = lax.axis_index("seq")
    first_row = position * row_count
    empty = jnp.zeros_like(own_gram)
    lower_gram, lower_cross = prefix((own_gram, own_cross), "seq", add_pair, (empty, empty), False)
    start_gram = prior_gram + lower_gram
    start_cross = prior_cross + lower_cross
    batched = jax.vmap(jax.checkpoint(block_forward), in_axes=(0, 0, 0, 0, 0, 0, None))

    def local_forward(first, second, third, fourth, fifth):
        return batched(first, second, third, fourth, fifth, ridge, first_row)

    outputs, pullback = jax.vjp(local_forward, head_q, head_k, head_v, start_gram, start_cross)
    mixed = join_heads(outputs)
    scaled_cot = gain * cotangent
    local_square = jnp.sum(mixed * mixed, axis=1)
    local_cross = jnp.sum(scaled_cot * mixed, axis=1)
    total_square = lax.psum(local_square, "head")
    feature_count = width * lax.axis_size("head")
    inverse = lax.rsqrt(total_square / feature_count + epsilon)[:, None]
    normed = mixed * inverse * gain
    total_cross = lax.psum(local_cross, "head")
    grad_mixed = (
        inverse * scaled_cot
        - mixed * (inverse * inverse * inverse) * (total_cross / feature_count)[:, None]
    )
    grad_q, grad_k, grad_v, grad_gram, grad_cross = pullback(split_heads(grad_mixed))
    later_gram, later_cross = prefix((grad_gram, grad_cross), "seq", add_pair, (empty, empty), True)
    symmetric = later_gram + jnp.transpose(later_gram, (0, 2, 1))
    grad_k = (
        grad_k
        + jnp.einsum("hti,hij->htj", head_k, symmetric, precision=highest)
        + jnp.einsum("htj,hij->hti", head_v, later_cross, precision=highest)
    )
    grad_v = grad_v + jnp.einsum("hti,hij->htj", head_k, later_cross, precision=highest)
    return (normed, join_heads(grad_q), join_heads(grad_k), join_heads(grad_v))


def solution(mesh):
    in_specs = (
        P("seq", "head"),
        P("seq", "head"),
        P("seq", "head"),
        P("head"),
        P("head"),
        P("head", None, None),
        P("head", None, None),
        P("seq", "head"),
    )
    out_specs = (P("seq", "head"), P("seq", "head"), P("seq", "head"), P("seq", "head"))
    return jax.shard_map(local, mesh=mesh, in_specs=in_specs, out_specs=out_specs, check_vma=False)
```

profile of v0, /device:TPU:1, one launch (start us, length us, event | category | flops | bytes accessed | tf_op | source)
XLA Modules:
  0.0 445.6 jit_solution(2497507912870803327)
XLA Ops:
  7.2 2.3 fusion.85
  9.7 2.2 fusion.86
  14.7 49.3 %all-gather.9.cloned.1.call-done = f32[4096,128]{1,0:T(8,128)} async-done(((f32[128,128]{1,0:T(8,128)}), f32[4096,128]{1,0:T(8,128)}) %all-gather.9.cloned.1.call-update) | async-done | bytes 2097168 | tf_op jit(solution)/shard_map/all_gather | solution.py:17
  63.9 51.1 %all-gather.11.cloned.1.call-done = f32[4096,128]{1,0:T(8,128)} async-done(((f32[128,128]{1,0:T(8,128)}), f32[4096,128]{1,0:T(8,128)}) %all-gather.11.cloned.1.call-update) | async-done | bytes 2097168 | tf_op jit(solution)/shard_map/all_gather | solution.py:17
  116.9 30.1 %while.107 = (s32[]{:T(128)}, f32[1,512,128]{1,2,0:T(8,128)S(1)}, f32[1,512,128]{1,2,0:T(8,128)S(1)}, f32[1,512,128]{1,2,0:T(8,128)S(1)}, f32[1,512,1]{1,2,0:T(1...) while((s32[]{:T(128)}, f32[1,512,128]{1,2,0:T(8,128)S(1)}, ...), condition=%wide.region_6.7_spmd.clone, body=%wide.region_3.6_spmd.clone.sunk | while | flops 907675648 | bytes 6125703 | solution.py:56
  117.9 1.2 fusion.135
  121.7 1.2 fusion.135
  125.5 1.2 fusion.135
  133.0 1.2 fusion.135
  149.8 13.8 %all-reduce = (f32[512]{0:T(512)S(1)}, f32[512]{0:T(512)S(1)}) all-reduce(f32[512]{0:T(512)S(1)} %get-tuple-element.1178, f32[512]{0:T(512)S(1)} %get-tuple-element.1177), channel_id=1, replica_groups=mesh['seq'=32,'head'=8] {'head'}, use_global_device_ids=true, to_apply=%region_8.9 | all-reduce | flops 1024 | bytes 8192 | tf_op jit(solution)/shard_map/psum | solution.py:99
  164.9 63.0 %while.108 = (s32[]{:T(128)}, f32[1,512,128]{1,2,0:T(8,128)S(1)}, f32[1,512,128]{1,2,0:T(8,128)S(1)}, f32[1,512,128]{1,2,0:T(8,128)S(1)}, f32[1,512,1]{1,2,0:T(1...) while((s32[]{:T(128)}, f32[1,512,128]{1,2,0:T(8,128)S(1)}, ...), condition=%wide.region_15.16_spmd.clone, body=%wide.region_12.15_spmd.clone.sunk | while | flops 907677696 | bytes 8506591 | solution.py:56
  164.9 2.0 bitcast_dynamic-update-slice_fusion.6
  172.8 2.0 bitcast_dynamic-update-slice_fusion.6
  180.7 2.0 bitcast_dynamic-update-slice_fusion.6
  188.5 2.0 bitcast_dynamic-update-slice_fusion.6
  196.4 2.0 bitcast_dynamic-update-slice_fusion.6
  204.2 2.0 bitcast_dynamic-update-slice_fusion.6
  212.1 2.0 bitcast_dynamic-update-slice_fusion.6
  219.9 2.0 bitcast_dynamic-update-slice_fusion.6
  232.8 99.0 %while.109 = (s32[]{:T(128)}, f32[1,512,128]{1,2,0:T(8,128)S(1)}, f32[1,128,128]{1,2,0:T(8,128)S(1)}, f32[1,512,128]{2,1,0:T(8,128)S(1)}, f32[1,512,128]{2,1,0:T...) while((s32[]{:T(128)}, f32[1,512,128]{1,2,0:T(8,128)S(1)}, ...), condition=%wide.region_20.21_spmd.clone, body=%wide.region_16.20_spmd.clone.sunk | while | flops 1814796800 | bytes 15208740 | solution.py:56
  241.9 2.0 fusion.155
  254.2 2.0 fusion.155
  266.6 2.0 fusion.155
  278.9 2.0 fusion.155
  291.3 2.0 fusion.155
  303.7 2.0 fusion.155
  316.1 2.0 fusion.155
  328.5 2.0 fusion.155
  332.7 1.8 copy.75
  337.1 1.8 fusion.64
  339.0 69.1 %all-gather.13.cloned.1.call-done = f32[32,128,128]{2,1,0:T(8,128)} async-done(((f32[1,128,128]{2,1,0:T(8,128)}), f32[32,128,128]{2,1,0:T(8,128)}) %all-gather.13.cloned.1.call-update) | async-done | bytes 2097168 | tf_op jit(solution)/shard_map/all_gather | solution.py:17
  408.1 28.2 %while.106 = (s32[]{:T(128)}, f32[1,128,128]{2,1,0:T(8,128)S(1)}, f32[1,128,128]{2,1,0:T(8,128)S(1)}, s32[]{:T(128)}, f32[32,1,128,128]{3,2,1,0:T(8,128)}, /*ind...) while((s32[]{:T(128)}, f32[1,128,128]{2,1,0:T(8,128)S(1)}, ...), condition=%wide.region_22.23_spmd, body=%wide.region_21.22_spmd.sunk | while | flops 32774 | bytes 393367 | solution.py:26
  (426 shorter events, 201.3 us)
Async XLA Ops:
  7.2 2.5 copy-start
  7.2 7.3 %copy-start.4 = (f32[512,128]{1,0:T(8,128)S(1)}, f32[512,128]{1,0:T(8,128)}, u32[]{:S(2)}) copy-start(f32[512,128]{1,0:T(8,128)} %param.18) | copy-start | bytes 786436
  7.2 7.2 %copy-start.8 = (f32[512,128]{1,0:T(8,128)S(1)}, f32[512,128]{1,0:T(8,128)}, u32[]{:S(2)}) copy-start(f32[512,128]{1,0:T(8,128)} %param.25) | copy-start | bytes 786436
  7.2 56.7 %all-gather.9.cloned.1.call-start = ((), (), s32[]{:S(2)}) async-start(), calls=%async_computation | async-start | bytes 2162688 | tf_op jit(solution)/shard_map/all_gather | solution.py:17
  9.6 105.5 %all-gather.11.cloned.1.call-start = ((), (), s32[]{:S(2)}) async-start(), calls=%async_computation.1 | async-start | bytes 2162688 | tf_op jit(solution)/shard_map/all_gather | solution.py:17
  11.9 327.1 %all-gather.15.cloned.1.call-start = ((), (), s32[]{:S(2)}) async-start(), calls=%async_computation.3 | async-start | bytes 2162688 | tf_op jit(solution)/shard_map/all_gather | solution.py:17
  13.2 103.7 %copy-start.1 = (f32[512,128]{1,0:T(8,128)S(1)}, f32[512,128]{1,0:T(8,128)}, u32[]{:S(2)}) copy-start(f32[512,128]{1,0:T(8,128)} %param.19) | copy-start | bytes 786436
  147.0 2.3 copy-start.10
  147.0 2.3 copy-start.11
  164.4 67.8 %copy-start.6 = (f32[1,512,128]{1,2,0:T(8,128)}, f32[1,512,128]{1,2,0:T(8,128)S(1)}, u32[]{:S(2)}) copy-start(f32[1,512,128]{1,2,0:T(8,128)S(1)} %get-tuple-element.759) | copy-start | bytes 786436
  228.2 4.6 %copy-start.9 = (f32[1,512,1]{1,2,0:T(1,128)S(1)}, f32[1,512,1]{1,2,0:T(1,128)}, u32[]{:S(2)}) copy-start(f32[1,512,1]{1,2,0:T(1,128)} %custom-call.6) | copy-start | bytes 6148
  229.0 179.1 %all-gather.13.cloned.1.call-start = ((), (), s32[]{:S(2)}) async-start(), calls=%async_computation.2 | async-start | bytes 2162688 | tf_op jit(solution)/shard_map/all_gather | solution.py:17
  230.2 1.0 copy-start.2
  331.8 3.7 copy-start.7
  332.6 3.7 copy-start.5
  334.5 2.6 copy-start.3
Sparse Core Ops, SparseCore 0:
  11.1 52.7 all-gather.8
  67.1 47.9 all-gather.10
  229.1 75.3 all-gather.14
  332.7 75.3 all-gather.12
where the time goes:
time: 449 us; the launch traced here: 446 us
  waiting for transfers between devices  170 us (38%)
  matrix products  112 us (25%)
  other arithmetic  89.9 us (20%)
  local copies, waits for them, and re-layouts  42.8 us (10%)
  between operations  14.3 us (3%)
  blocking collectives  13.8 us (3%)
    all_gather x4, waiting for transfers between devices, prefix(): gathered = jax.tree.map(lambda a: lax.all_gather(a, axis), part)  169 us
    dot_general x32, matrix products, apply_system(): jnp.dot(inner, keyset, precision=highest)  43.5 us
    dot_general x32, matrix products, apply_system(): inner = jnp.dot(search, keyset.T, precision=highest) * causal  38 us
    dynamic_slice x56, local copies, waits for them, and re-layouts, block_forward(): (solution, _, _, _), _ = lax.scan(cg_step, start, None, length=ITERS)  30.2 us
    add x31, other arithmetic, add_pair(): return (earlier[0] + later[0], earlier[1] + later[1])  28.2 us
    dynamic_update_slice x32, other arithmetic, block_forward(): (solution, _, _, _), _ = lax.scan(cg_step, start, None, length=ITERS)  21.7 us
    mul x24, other arithmetic, block_forward(): ridge_value * (first_row + places + 1).astype(jnp.float32)[:, None]  15.7 us
    dot_general x32, matrix products, apply_system(): jnp.dot(search, start_gram, precision=highest)  15.3 us
  transfers between devices with their start and end apart: 4, of which 3 were waited for; matrix products, arithmetic and copies ran while one was open for 25% of the time, Pallas kernels for 0%

commit v1 on v0

v1 whole, which is shorter than its diff:
```python
import functools

import jax
import jax.numpy as jnp
from jax import lax
from jax.experimental import pallas as pl
from jax.experimental.pallas import tpu as pltpu
from jax.sharding import PartitionSpec as P

DH = 128
ITERS = 8
CH = 128
epsilon = 1e-06

F32 = jnp.float32
BF16 = jnp.bfloat16
MESH = pl.DeviceIdType.MESH


def left(x):
    hi = x.astype(BF16)
    lo = (x - hi.astype(F32)).astype(BF16)
    return jnp.concatenate([hi, lo], axis=1)


def right(halves):
    return jnp.concatenate([halves, halves], axis=0)


def right_t(halves):
    hi, lo = halves[:, :CH], halves[:, CH:]
    return jnp.concatenate(
        [jnp.concatenate([hi, hi], axis=1), jnp.concatenate([lo, lo], axis=1)], axis=0
    )


def fold(out):
    return out[:, :CH] + out[:, CH:]


def mul(a, b):
    return fold(jnp.dot(a, right(b), preferred_element_type=F32))


def mul_t(pairs):
    a = jnp.concatenate([pair[0] for pair in pairs], axis=1)
    b = jnp.concatenate([right_t(pair[1]) for pair in pairs], axis=1)
    return fold(
        lax.dot_general(a, b, (((1,), (1,)), ((), ())), preferred_element_type=F32)
    )


def colsum(x):
    return jnp.sum(x, axis=0, keepdims=True)


def kernel(
    n_seq, n_head, features,
    q_hbm, k_hbm, v_hbm, gain_ref, ridge_ref, pg_hbm, pc_hbm, cot_hbm,
    normed_hbm, gq_hbm, gk_hbm, gv_hbm,
    q_in, k_in, v_in, cot_in, pg_in, pc_in,
    ak, kt, vl, vtl, cl, ctl, mg, mc, qt, ct,
    pf, wf, rf, pl_, sl, wbl, sbl, al, be, rrs, pws,
    xt, mx, sxl, syl, yl, xb, pb, rb, rrb, dsy, dcc,
    nat, o_normed, o_gq, o_gk, o_gv,
    src, recv1, buf2, recv2, stat, stat_in,
    in_sem, out_sem, s1, r1, s2, r2, hs, hr,
):
    me = lax.axis_index("seq")
    my_head = lax.axis_index("head")
    n_own = n_seq // 2
    pr = DH // n_own
    nch = k_in.shape[0] // CH
    mine = me // 2
    core = me - 2 * mine

    loads = []
    for at, (source, target) in enumerate(
        ((k_hbm, k_in), (v_hbm, v_in), (q_hbm, q_in), (pg_hbm.at[0], pg_in),
         (pc_hbm.at[0], pc_in), (cot_hbm, cot_in))
    ):
        copy = pltpu.make_async_copy(source, target, in_sem.at[at])
        copy.start()
        loads.append(copy)

    barrier = pltpu.get_barrier_semaphore()

    def greet_seq(turn, carry):
        pl.semaphore_signal(
            barrier, inc=1, device_id={"seq": lax.rem(me + turn, n_seq)}, device_id_type=MESH
        )
        return carry

    def greet_head(turn, carry):
        pl.semaphore_signal(
            barrier, inc=1, device_id={"head": lax.rem(my_head + turn, n_head)},
            device_id_type=MESH,
        )
        return carry

    lax.fori_loop(1, n_seq, greet_seq, 0)
    lax.fori_loop(1, n_head, greet_head, 0)

    def bytes_wait(ref, count, sem):
        view = ref.at[pl.ds(0, count)]
        pltpu.make_async_copy(view, view, sem).wait()

    def send_first(x, parity):
        def one(turn, carry):
            piece = lax.rem(mine + turn, n_own)
            owner = 2 * piece + parity

            @pl.when(owner != me)
            def _():
                pltpu.make_async_remote_copy(
                    src_ref=src.at[x, piece], dst_ref=recv1.at[x, me],
                    send_sem=s1.at[x], recv_sem=r1.at[x],
                    device_id={"seq": owner}, device_id_type=MESH,
                ).start()

            return carry

        lax.fori_loop(0, n_own, one, 0)

        @pl.when(core == parity)
        def _():
            recv1[x, me] = src[x, mine]

    def send_second(x, parity, reverse, base):
        @pl.when(core == parity)
        def _():
            bytes_wait(recv1.at[x], n_seq - 1, r1.at[x])
            if base is None:
                total = jnp.zeros((pr, DH), F32)
            else:
                total = base[pl.ds(pl.multiple_of(mine * pr, pr), pr), :]
            order = range(n_seq - 1, -1, -1) if reverse else range(n_seq)
            for device in order:
                buf2[x, device] = total
                total = total + recv1[x, device]

            def one(turn, carry):
                device = lax.rem(me + turn, n_seq)
                pltpu.make_async_remote_copy(
                    src_ref=buf2.at[x, device], dst_ref=recv2.at[x, mine],
                    send_sem=s2.at[x], recv_sem=r2.at[x],
                    device_id={"seq": device}, device_id_type=MESH,
                ).start()
                return carry

            lax.fori_loop(1, n_seq, one, 0)
            recv2[x, mine] = buf2[x, me]

    def finish(x, parity):
        @pl.when(core == parity)
        def _():
            bytes_wait(recv2.at[x], n_own - 1, r2.at[x])

        @pl.when(core != parity)
        def _():
            bytes_wait(recv2.at[x], n_own, r2.at[x])

        return recv2[x].reshape(DH, DH)

    def drain(x, parity):
        @pl.when(core == parity)
        def _():
            bytes_wait(src.at[x], n_own - 1, s1.at[x])
            bytes_wait(buf2.at[x], n_seq - 1, s2.at[x])

        @pl.when(core != parity)
        def _():
            bytes_wait(src.at[x], n_own, s1.at[x])

    rows = [pl.ds(c * CH, CH) for c in range(nch)]
    keep = (
        lax.broadcasted_iota(jnp.int32, (CH, CH), 0)
        <= lax.broadcasted_iota(jnp.int32, (CH, CH), 1)
    )
    lane = lax.broadcasted_iota(jnp.int32, (1, CH), 1)
    first_row = me * k_in.shape[0]
    damping = [
        ridge_ref[0] * (first_row + (c * CH + 1) + lane).astype(F32) for c in range(nch)
    ]

    loads[0].wait()
    total = jnp.zeros((DH, DH), F32)
    for c in range(nch):
        keys = k_in[rows[c], :]
        halves = left(keys)
        halves_t = left(keys.T)
        ak[c, DH:, :] = halves
        kt[c] = halves_t
        gram = mul(halves_t, halves)
        mg[c] = gram
        total = total + gram
    src[0] = total.reshape(n_own, pr, DH)
    pl.semaphore_wait(barrier, n_seq - 1 + n_head - 1)
    send_first(0, 0)

    loads[1].wait()
    total = jnp.zeros((DH, DH), F32)
    for c in range(nch):
        values = v_in[rows[c], :]
        halves = left(values)
        vl[c] = halves
        cross = mul(kt[c], halves)
        mc[c] = cross
        total = total + cross
    src[1] = total.reshape(n_own, pr, DH)
    send_first(1, 1)
    loads[3].wait()
    loads[4].wait()
    send_second(0, 0, False, pg_in)
    send_second(1, 1, False, pc_in)

    loads[2].wait()
    loads[5].wait()
    for c in range(nch):
        vtl[c] = left(v_in[rows[c], :].T)
        qt[c] = q_in[rows[c], :].T
        ct[c] = (cot_in[rows[c], :] * gain_ref[...]).T

    def apply_system(c, halves, search):
        both = fold(jnp.dot(ak[c], right(halves), preferred_element_type=F32))
        inner = left(jnp.where(keep, both[DH:], 0.0))
        return both[:DH] + mul(kt[c], inner) + damping[c] * search, inner

    gram = finish(0, 0)
    for c in range(nch):
        ak[c, :DH, :] = left(gram)
        if c + 1 < nch:
            gram = gram + mg[c]

    for c in range(nch):
        start = qt[c]
        pf[0, c] = start
        pl_[0, c] = left(start)
        rrs[0, c : c + 1, :] = colsum(start * start)
        xt[c] = jnp.zeros_like(start)

    def forward(step, carry):
        for c in range(nch):
            search = pf[step, c]
            image, inner = apply_system(c, pl_[step, c], search)
            wf[step, c] = image
            sl[step, c] = inner
            squared = rrs[step, c : c + 1, :]
            curve = colsum(search * image)
            alpha = squared / curve
            pws[step, c : c + 1, :] = curve
            al[step, c : c + 1, :] = alpha
            xt[c] = xt[c] + alpha * search
            before = qt[c]
            residual = before - alpha * image
            qt[c] = residual
            rf[step, c] = residual
            squared_next = colsum(residual * residual)
            beta = squared_next / squared
            be[step, c : c + 1, :] = beta
            rrs[step + 1, c : c + 1, :] = squared_next
            search = residual + beta * search
            pf[step + 1, c] = search
            pl_[step + 1, c] = left(search)
        return carry

    lax.fori_loop(0, ITERS, forward, 0)

    cross = finish(1, 1)
    for c in range(nch):
        cl[c] = left(cross)
        ctl[c] = left(cross.T)
        if c + 1 < nch:
            cross = cross + mc[c]
    for c in range(nch):
        halves = left(xt[c])
        inner = left(jnp.where(keep, mul(ak[c, DH:, :], halves), 0.0))
        sxl[c] = inner
        mixed = mul(ctl[c], halves) + mul(vtl[c], inner)
        mx[c] = mixed
        stat[c : c + 1, :] = colsum(mixed * mixed)
        stat[nch + c : nch + c + 1, :] = colsum(ct[c] * mixed)

    def send_stat(turn, carry):
        device = lax.rem(my_head + turn, n_head)
        pltpu.make_async_remote_copy(
            src_ref=stat, dst_ref=stat_in.at[my_head], send_sem=hs.at[0], recv_sem=hr.at[0],
            device_id={"head": device}, device_id_type=MESH,
        ).start()
        return carry

    lax.fori_loop(1, n_head, send_stat, 0)
    stat_in[my_head] = stat[...]
    bytes_wait(stat_in, n_head - 1, hr.at[0])
    sums = stat_in[0]
    for device in range(1, n_head):
        sums = sums + stat_in[device]
    inverse = lax.rsqrt(sums[:nch] / features + epsilon)
    pull = inverse * inverse * inverse * (sums[nch:] / features)

    total = jnp.zeros((DH, DH), F32)
    for c in range(nch):
        scale = inverse[c : c + 1, :]
        mixed = mx[c]
        o_normed[rows[c], :] = (mixed * scale).T * gain_ref[...]
        grad = left(scale * ct[c] - mixed * pull[c : c + 1, :])
        yl[c] = grad
        inner = left(jnp.where(keep, mul(vl[c], grad), 0.0))
        syl[c] = inner
        xb[c] = mul(cl[c], grad) + mul(kt[c], inner)
        part = mul_t([(left(xt[c]), grad)])
        dcc[c] = part
        total = total + part
    src[3] = total.reshape(n_own, pr, DH)
    send_first(3, 1)
    stores = [pltpu.make_async_copy(o_normed, normed_hbm, out_sem.at[0])]
    stores[0].start()

    last = ITERS - 1
    for c in range(nch):
        search, image, solution_bar = pf[last, c], wf[last, c], xb[c]
        alpha, curve = al[last, c : c + 1, :], pws[last, c : c + 1, :]
        alpha_bar = colsum(solution_bar * search)
        curve_bar = -alpha_bar * alpha / curve
        wbl[last, c] = left(curve_bar * search)
        halves = sl[last, c]
        sbl[last, c] = left(
            curve_bar * (halves[:, :CH].astype(F32) + halves[:, CH:].astype(F32))
        )
        pb[c] = alpha * solution_bar + 2.0 * curve_bar * image
        rb[c] = jnp.zeros((DH, CH), F32)
        rrb[c : c + 1, :] = alpha_bar / curve

    def backward(turn, carry):
        step = last - 1 - turn
        for c in range(nch):
            search, image, solution_bar = pf[step, c], wf[step, c], xb[c]
            alpha, curve = al[step, c : c + 1, :], pws[step, c : c + 1, :]
            beta, squared = be[step, c : c + 1, :], rrs[step, c : c + 1, :]
            search_bar = pb[c]
            beta_bar = colsum(search_bar * search) / squared
            next_bar = rrb[c : c + 1, :] + beta_bar
            residual_bar = rb[c] + search_bar + (2.0 * next_bar) * rf[step, c]
            alpha_bar = colsum(solution_bar * search - residual_bar * image)
            ratio = alpha_bar / curve
            curve_bar = -ratio * alpha
            image_bar = curve_bar * search - alpha * residual_bar
            halves = left(image_bar)
            wbl[step, c] = halves
            moved, inner = apply_system(c, halves, image_bar)
            sbl[step, c] = inner
            pb[c] = beta * search_bar + alpha * solution_bar + curve_bar * image + moved
            rb[c] = residual_bar
            rrb[c : c + 1, :] = ratio - beta_bar * beta
        return carry

    lax.fori_loop(0, last, backward, 0)

    total = jnp.zeros((DH, DH), F32)
    for c in range(nch):
        part = mul_t([(pl_[j, c], wbl[j, c]) for j in range(ITERS)])
        part = part + part.T
        dsy[c] = part
        total = total + part
    src[2] = total.reshape(n_own, pr, DH)
    send_first(2, 0)
    send_second(3, 1, True, None)

    for c in range(nch):
        first = q_in[rows[c], :].T
        grad = rb[c] + pb[c] + 2.0 * rrb[c : c + 1, :] * first
        o_gq[rows[c], :] = grad.T
    stores.append(pltpu.make_async_copy(o_gq, gq_hbm, out_sem.at[1]))
    stores[1].start()
    send_second(2, 0, True, None)
    for c in range(nch):
        pairs = [(syl[c], left(xt[c]))]
        for j in range(ITERS):
            pairs.append((sl[j, c], wbl[j, c]))
            pairs.append((sbl[j, c], pl_[j, c]))
        o_gk[rows[c], :] = mul_t(pairs)
        o_gv[rows[c], :] = mul_t([(sxl[c], yl[c])])

    cross = finish(3, 1)
    for c in range(nch - 1, -1, -1):
        halves = left(cross)
        o_gv[rows[c], :] += mul(ak[c, DH:, :], halves)
        o_gk[rows[c], :] += mul_t([(vl[c], halves)])
        cross = cross + dcc[c]
    stores.append(pltpu.make_async_copy(o_gv, gv_hbm, out_sem.at[3]))
    stores[2].start()
    gram = finish(2, 0)
    for c in range(nch - 1, -1, -1):
        o_gk[rows[c], :] += mul(ak[c, DH:, :], left(gram))
        gram = gram + dsy[c]
    stores.append(pltpu.make_async_copy(o_gk, gk_hbm, out_sem.at[2]))
    stores[3].start()

    bytes_wait(stat_in, n_head - 1, hs.at[0])
    drain(0, 0)
    drain(1, 1)
    drain(2, 0)
    drain(3, 1)
    for copy in stores:
        copy.wait()


def local(n_seq, n_head, queries, keys, values, gain, ridge, prior_gram, prior_cross, cotangent):
    rows, width = queries.shape
    nch = rows // CH
    n_own = n_seq // 2
    pr = DH // n_own
    anyspace = pl.BlockSpec(memory_space=pl.ANY)
    vmem = pl.BlockSpec(memory_space=pltpu.VMEM)
    smem = pl.BlockSpec(memory_space=pltpu.SMEM)
    tok = pltpu.VMEM((rows, DH), F32)
    square = pltpu.VMEM((DH, DH), F32)
    per_chunk = pltpu.VMEM((nch, DH, CH), F32)
    halves = pltpu.VMEM((nch, DH, 2 * CH), BF16)
    per_step = pltpu.VMEM((ITERS, nch, DH, CH), F32)
    step_halves = pltpu.VMEM((ITERS, nch, DH, 2 * CH), BF16)
    scal = pltpu.VMEM((ITERS + 1, nch, CH), F32)
    scratch = [
        tok, tok, tok, tok, square, square,
        pltpu.VMEM((nch, 2 * DH, 2 * CH), BF16), halves, halves, halves, halves, halves,
        per_chunk, per_chunk, per_chunk, per_chunk,
        pltpu.VMEM((ITERS + 1, nch, DH, CH), F32), per_step, per_step,
        pltpu.VMEM((ITERS + 1, nch, DH, 2 * CH), BF16), step_halves, step_halves, step_halves,
        scal, scal, scal, scal,
        per_chunk, per_chunk, halves, halves, halves, per_chunk, per_chunk, per_chunk,
        pltpu.VMEM((nch, CH), F32), per_chunk, per_chunk,
        tok, tok, tok, tok, tok,
        pltpu.VMEM((4, n_own, pr, DH), F32), pltpu.VMEM((4, n_seq, pr, DH), F32),
        pltpu.VMEM((4, n_seq, pr, DH), F32), pltpu.VMEM((4, n_own, pr, DH), F32),
        pltpu.VMEM((2 * nch, CH), F32), pltpu.VMEM((n_head, 2 * nch, CH), F32),
        pltpu.SemaphoreType.DMA((6,)), pltpu.SemaphoreType.DMA((4,)),
        pltpu.SemaphoreType.DMA((4,)), pltpu.SemaphoreType.DMA((4,)),
        pltpu.SemaphoreType.DMA((4,)), pltpu.SemaphoreType.DMA((4,)),
        pltpu.SemaphoreType.DMA((1,)), pltpu.SemaphoreType.DMA((1,)),
    ]
    shape = jax.ShapeDtypeStruct((rows, width), F32)
    return pl.pallas_call(
        functools.partial(kernel, n_seq, n_head, float(width * n_head)),
        out_shape=(shape, shape, shape, shape),
        in_specs=[anyspace, anyspace, anyspace, vmem, smem, anyspace, anyspace, anyspace],
        out_specs=(anyspace, anyspace, anyspace, anyspace),
        scratch_shapes=scratch,
        compiler_params=pltpu.CompilerParams(
            collective_id=0, has_side_effects=True, vmem_limit_bytes=60 * 1024 * 1024
        ),
    )(queries, keys, values, gain.reshape(1, width), ridge, prior_gram, prior_cross, cotangent)


def solution(mesh):
    in_specs = (
        P("seq", "head"),
        P("seq", "head"),
        P("seq", "head"),
        P("head"),
        P("head"),
        P("head", None, None),
        P("head", None, None),
        P("seq", "head"),
    )
    out_specs = (P("seq", "head"), P("seq", "head"), P("seq", "head"), P("seq", "head"))
    body = functools.partial(local, mesh.shape["seq"], mesh.shape["head"])
    return jax.shard_map(body, mesh=mesh, in_specs=in_specs, out_specs=out_specs, check_vma=False)
```

time: 449 us -> 65.2 us (0.15)
  waiting for transfers between devices: 170 us -> 0 us
  matrix products: 112 us -> 0 us
  other arithmetic: 89.9 us -> 0 us
  Pallas kernels: 0 us -> 59.2 us
  local copies, waits for them, and re-layouts: 42.8 us -> 4.5 us
  blocking collectives: 13.8 us -> 0 us
  between operations: 14.3 us -> 1.3 us
    all_gather x4 -> x0, waiting for transfers between devices: 169 us -> none  [prefix(): gathered = jax.tree.map(lambda a: lax.all_gather(a, axis), part)]
    dot_general x111 -> x0, matrix products: 112 us -> none  [the longest x32 43.5 us: apply_system(): jnp.dot(inner, keyset, precision=highest)]
    pallas_call x0 -> x1, Pallas kernels: none -> 59.2 us  [local(): pl.pallas_call(functools.partial(kernel, n_seq, n_head, float(width * n_h...]
    add x49 -> x0, other arithmetic: 31.8 us -> none  [the longest x31 28.2 us: add_pair(): return (earlier[0] + later[0], earlier[1] + later[1])]
    dynamic_slice x56 -> x0, local copies, waits for them, and re-layouts: 30.2 us -> none  [block_forward(): (solution, _, _, _), _ = lax.scan(cg_step, start, None, length=ITERS)]
    dynamic_update_slice x32 -> x0, other arithmetic: 21.7 us -> none  [block_forward(): (solution, _, _, _), _ = lax.scan(cg_step, start, None, length=ITERS)]
    mul x25 -> x0, other arithmetic: 15.7 us -> none  [the longest x24 15.7 us: block_forward(): ridge_value * (first_row + places + 1).astype(jnp.float32)[:, None]]
    psum x1 -> x0, blocking collectives: 13.8 us -> none  [local(): total_square = lax.psum(local_square, 'head')]
  transfers between devices with their start and end apart: 4 -> 0, of which waited for: 3 -> 0; matrix products, arithmetic and copies ran while one was open for 25% -> 0% of each run, Pallas kernels for 0% -> 0%
where the time goes in v1:
time: 65.2 us; the launch traced here: 65 us
  Pallas kernels  59.2 us (91%)
  local copies, waits for them, and re-layouts  4.5 us (7%)
  between operations  1.3 us (2%)
    pallas_call x1, Pallas kernels, local(): pl.pallas_call(functools.partial(kernel, n_seq, n_head, float(width * n_h...  59.2 us
    unnamed x10, local copies, waits for them, and re-layouts  4.5 us

profile of v1, /device:TPU:1, one launch (start us, length us, event | category | flops | bytes accessed | tf_op | source)
XLA Modules:
  0.0 65.0 jit_solution(4663254626096809316)
XLA Ops:
  1.3 59.2 %shard_map.111 = (f32[512,128]{1,0:T(8,128)}, f32[512,128]{1,0:T(8,128)}, f32[512,128]{1,0:T(8,128)}, f32[512,128]{1,0:T(8,128)}) custom-call(f32[512,128]{1,0:T(8,128)} %q_hbm.1, f32[512,128]{1,0:T(8,128)} %k_hbm.1, f32[512,128]{1,0:T(8,128)} %v_hbm.1, f32[1,128]{1,0:T(1,128)} %bitcast.1, f32[1]{0:T(128)S(6)} %copy.16.ridge_ref, f32[1,128,128]{2,1,0:T(8,128)} %pg_hbm.1, ...), custom_call_target="tpu_custom_call" | custom-call | tf_op jit(solution)/shard_map/pallas_call | solution.py:442
  60.4 0.0 copy-start.2
  60.5 1.7 %copy.17 = f32[512,128]{1,0:T(8,128)} copy(f32[512,128]{1,0:T(8,128)} %get-tuple-element.8) | data formatting | bytes 524288
  62.2 0.0 copy-done.2
  62.2 0.0 copy-start.1
  62.2 0.7 %copy.18 = f32[512,128]{1,0:T(8,128)} copy(f32[512,128]{1,0:T(8,128)S(1)} %copy-done.2) | data formatting | bytes 524288
  62.9 0.3 copy-done.1
  63.2 0.0 copy-start
  63.2 0.7 %copy.19 = f32[512,128]{1,0:T(8,128)} copy(f32[512,128]{1,0:T(8,128)S(1)} %copy-done.1) | data formatting | bytes 524288
  63.9 0.3 copy-done
  64.3 0.7 %copy.20 = f32[512,128]{1,0:T(8,128)} copy(f32[512,128]{1,0:T(8,128)S(1)} %copy-done) | data formatting | bytes 524288
Async XLA Ops:
  60.4 1.7 %copy-start.2 = (f32[512,128]{1,0:T(8,128)S(1)}, f32[512,128]{1,0:T(8,128)}, u32[]{:S(2)}) copy-start(f32[512,128]{1,0:T(8,128)} %get-tuple-element.9) | copy-start | bytes 786436
  62.2 1.0 %copy-start.1 = (f32[512,128]{1,0:T(8,128)S(1)}, f32[512,128]{1,0:T(8,128)}, u32[]{:S(2)}) copy-start(f32[512,128]{1,0:T(8,128)} %get-tuple-element.10) | copy-start | bytes 786436
  63.2 1.0 %copy-start = (f32[512,128]{1,0:T(8,128)S(1)}, f32[512,128]{1,0:T(8,128)}, u32[]{:S(2)}) copy-start(f32[512,128]{1,0:T(8,128)} %get-tuple-element.11) | copy-start | bytes 786436

commit v2 on v0

v2 whole, which is shorter than its diff:
```python
import functools

import jax
import jax.numpy as jnp
from jax import lax
from jax.experimental import pallas as pl
from jax.experimental.pallas import tpu as pltpu
from jax.sharding import PartitionSpec as P

DH = 128
ITERS = 8
CH = 128
epsilon = 1e-06

F32 = jnp.float32
BF16 = jnp.bfloat16
MESH = pl.DeviceIdType.MESH


def left(x):
    hi = x.astype(BF16)
    lo = (x - hi.astype(F32)).astype(BF16)
    return jnp.concatenate([hi, lo], axis=1)


def right(halves):
    return jnp.concatenate([halves, halves], axis=0)


def fold(out):
    return out[:, :CH] + out[:, CH:]


def mul(a, b):
    return fold(jnp.dot(a, right(b), preferred_element_type=F32))


def mul_cat(pairs):
    a = jnp.concatenate([pair[0] for pair in pairs], axis=1)
    b = jnp.concatenate([right(pair[1]) for pair in pairs], axis=0)
    return fold(jnp.dot(a, b, preferred_element_type=F32))


def stack(parts):
    his = jnp.concatenate([part[:, :CH] for part in parts], axis=1)
    los = jnp.concatenate([part[:, CH:] for part in parts], axis=1)
    return jnp.concatenate([his, los], axis=0)


def mul_t(pairs):
    out = fold(
        lax.dot_general(
            stack([pair[0] for pair in pairs]), stack([pair[1] for pair in pairs]),
            (((1,), (1,)), ((), ())), preferred_element_type=F32,
        )
    )
    return out[:DH] + out[DH:]


def colsum(x):
    while x.shape[0] > 8:
        half = x.shape[0] // 2
        x = x[:half] + x[half:]
    for shift in (4, 2, 1):
        x = x + pltpu.roll(x, shift, 0)
    return x


def scaled(row, x):
    return (x.reshape(-1, 8, CH) * row).reshape(x.shape)


def interleave(makers, offsets):
    chains = [(maker, late) for maker, late in zip(makers, offsets)]
    turn = 0
    while chains:
        left_over = []
        for chain, late in chains:
            if turn < late or next(chain, True) is None:
                left_over.append((chain, late))
        chains = left_over
        turn += 1


def hops(offset):
    return (0, 1, 2, 1)[offset]


def kernel(
    n_seq, n_head, features,
    q_hbm, k_hbm, v_hbm, gain_hbm, ridge_hbm, pg_hbm, pc_hbm, cot_hbm,
    o_normed, o_gq, o_gk, o_gv,
    q_in, k_in, v_in, cot_in, pg_in, pc_in, gain_in, ridge_in,
    ak, kt, vl, vtl, cl, ctl, mg, mc, qt, ct,
    pf, wf, rf, pl_, sl, wbl, sbl, al, be, rrs, pws, ivs,
    xt, xl, mx, sxl, syl, yl, xb, pb, rb, rrb, dsy, dcc,
    src, recv1, buf2, recv2, stat, stat_in,
    in_sem, s1, r1, s2, r2, hs, hr,
):
    me = lax.axis_index("seq")
    my_head = lax.axis_index("head")
    pr = DH // n_seq
    nch = k_in.shape[0] // CH

    pr8 = max(pr, 8)
    own_rows = pl.ds(pl.multiple_of(me * pr // pr8 * pr8, pr8), pr8)
    loads = []
    for at, (source, target) in enumerate(
        ((k_hbm, k_in), (v_hbm, v_in), (q_hbm, q_in), (pg_hbm.at[0, own_rows], pg_in),
         (pc_hbm.at[0, own_rows], pc_in), (cot_hbm, cot_in), (gain_hbm, gain_in),
         (ridge_hbm, ridge_in))
    ):
        copy = pltpu.make_async_copy(source, target, in_sem.at[at])
        copy.start()
        loads.append(copy)

    barrier = pltpu.get_barrier_semaphore()

    def greet_seq(turn, carry):
        pl.semaphore_signal(
            barrier, inc=1, device_id={"seq": lax.rem(me + turn, n_seq)}, device_id_type=MESH
        )
        return carry

    def greet_head(turn, carry):
        pl.semaphore_signal(
            barrier, inc=1, device_id={"head": lax.rem(my_head + turn, n_head)},
            device_id_type=MESH,
        )
        return carry

    lax.fori_loop(1, n_seq, greet_seq, 0)
    lax.fori_loop(1, n_head, greet_head, 0)

    if n_seq == 32:
        offsets = [(x, y, z) for x in range(4) for y in range(4) for z in range(2)]
        offsets = sorted(offsets, key=lambda o: -(hops(o[0]) + hops(o[1])))
        my_x, my_y, my_core = me // 8, lax.rem(me // 2, 4), lax.rem(me, 2)
        others = [
            lax.rem(my_x + x, 4) * 8 + lax.rem(my_y + y, 4) * 2 + lax.rem(my_core + z, 2)
            for x, y, z in offsets
            if (x, y, z) != (0, 0, 0)
        ]
    else:
        others = [lax.rem(me + turn, n_seq) for turn in range(1, n_seq)]
    turns = sorted(range(1, n_head), key=lambda turn: -min(turn, n_head - turn))

    def bytes_wait(ref, count, sem):
        view = ref.at[pl.ds(0, count)]
        pltpu.make_async_copy(view, view, sem).wait()

    def send(x, source, target, send_sem, recv_sem):
        for device in others:
            pltpu.make_async_remote_copy(
                src_ref=source.at[x, device], dst_ref=target.at[x, me],
                send_sem=send_sem.at[x], recv_sem=recv_sem.at[x],
                device_id={"seq": device}, device_id_type=MESH,
            ).start()
        target[x, me] = source[x, me]

    def send_first(x, total):
        src[x] = total.reshape(n_seq, pr, DH)
        send(x, src, recv1, s1, r1)

    def send_second(x, reverse, base):
        bytes_wait(recv1.at[x], n_seq - 1, r1.at[x])
        if base is None:
            total = jnp.zeros((pr, DH), F32)
        elif pr < 8:
            total = base[:pr]
            for part in range(1, 8 // pr):
                total = jnp.where(
                    lax.rem(me, 8 // pr) == part, base[part * pr : (part + 1) * pr], total
                )
        else:
            total = base[...]
        for device in range(n_seq - 1, -1, -1) if reverse else range(n_seq):
            buf2[x, device] = total
            total = total + recv1[x, device]
        send(x, buf2, recv2, s2, r2)

    def finish(x):
        bytes_wait(recv2.at[x], n_seq - 1, r2.at[x])
        return recv2[x].reshape(DH, DH)

    rows = [pl.ds(c * CH, CH) for c in range(nch)]
    keep = (
        lax.broadcasted_iota(jnp.int32, (CH, CH), 0)
        <= lax.broadcasted_iota(jnp.int32, (CH, CH), 1)
    )
    lane = lax.broadcasted_iota(jnp.int32, (8, CH), 1)
    first_row = me * k_in.shape[0]

    loads[0].wait()
    for c in range(nch):
        keys = k_in[rows[c], :]
        ak[c, DH:, :] = left(keys)
        kt[c] = left(keys.T)
    total = mul_cat([(kt[c], ak[c, DH:, :]) for c in range(nch)])
    pl.semaphore_wait(barrier, n_seq - 1 + n_head - 1)
    send_first(0, total)

    loads[1].wait()
    for c in range(nch):
        vl[c] = left(v_in[rows[c], :])
    send_first(1, mul_cat([(kt[c], vl[c]) for c in range(nch)]))

    loads[7].wait()
    damping = [
        ridge_in[0] * (first_row + (c * CH + 1) + lane).astype(F32) for c in range(nch)
    ]
    loads[2].wait()
    for c in range(nch):
        start = q_in[rows[c], :].T
        pf[0, c] = start
        pl_[0, c] = left(start)
        rrs[0, c] = colsum(start * start)
        xt[c] = jnp.zeros_like(start)
    for c in range(nch - 1):
        mg[c] = mul(kt[c], ak[c, DH:, :])
    loads[3].wait()
    send_second(0, False, pg_in)
    for c in range(nch - 1):
        mc[c] = mul(kt[c], vl[c])
    loads[4].wait()
    send_second(1, False, pc_in)
    loads[5].wait()
    loads[6].wait()
    for c in range(nch):
        vtl[c] = left(v_in[rows[c], :].T)
        ct[c] = (cot_in[rows[c], :] * gain_in[...]).T

    gram = finish(0)
    for c in range(nch):
        ak[c, :DH, :] = left(gram)
        if c + 1 < nch:
            gram = gram + mg[c]

    def forward(c):
        for step in range(ITERS):
            both = fold(jnp.dot(ak[c], right(pl_[step, c]), preferred_element_type=F32))
            yield
            inner = left(jnp.where(keep, both[DH:], 0.0))
            sl[step, c] = inner
            yield
            image = both[:DH] + mul(kt[c], inner)
            yield
            search = pf[step, c]
            image = image + scaled(damping[c], search)
            wf[step, c] = image
            curve = 1.0 / colsum(search * image)
            squared = rrs[step, c]
            alpha = squared * curve
            inv = 1.0 / squared
            pws[step, c] = curve
            al[step, c] = alpha
            ivs[step, c] = inv
            yield
            xt[c] = xt[c] + scaled(alpha, search)
            if step + 1 < ITERS:
                before = pf[0, c] if step == 0 else rf[step - 1, c]
                residual = before - scaled(alpha, image)
                rf[step, c] = residual
                squared = colsum(residual * residual)
                beta = squared * inv
                be[step, c] = beta
                rrs[step + 1, c] = squared
                search = residual + scaled(beta, search)
                pf[step + 1, c] = search
                pl_[step + 1, c] = left(search)
            else:
                xl[c] = left(xt[c])
            yield

    interleave([forward(c) for c in range(nch)], (0,1,3,4))

    cross = finish(1)
    for c in range(nch):
        ctl[c] = left(cross.T)
        cl[c] = left(cross)
        if c + 1 < nch:
            cross = cross + mc[c]

    def read_out(c):
        inner = mul(ak[c, DH:, :], xl[c])
        yield
        inner = left(jnp.where(keep, inner, 0.0))
        sxl[c] = inner
        yield
        mixed = mul_cat([(ctl[c], xl[c]), (vtl[c], inner)])
        yield
        mx[c] = mixed
        stat[c : c + 1, :] = colsum(mixed * mixed)[:1]
        stat[nch + c : nch + c + 1, :] = colsum(ct[c] * mixed)[:1]
        yield

    interleave([read_out(c) for c in range(nch)], range(nch))

    for turn in turns:
        pltpu.make_async_remote_copy(
            src_ref=stat, dst_ref=stat_in.at[my_head], send_sem=hs.at[0], recv_sem=hr.at[0],
            device_id={"head": lax.rem(my_head + turn, n_head)}, device_id_type=MESH,
        ).start()
    stat_in[my_head] = stat[...]
    bytes_wait(stat_in, n_head - 1, hr.at[0])
    sums = stat_in[0]
    for device in range(1, n_head):
        sums = sums + stat_in[device]
    inverse = lax.rsqrt(sums[:nch] / features + epsilon)
    pull = inverse * inverse * inverse * (sums[nch:] / features)

    last = ITERS - 1

    def backward(c):
        grad = left(inverse[c : c + 1, :] * ct[c] - mx[c] * pull[c : c + 1, :])
        yl[c] = grad
        inner = mul(vl[c], grad)
        yield
        inner = left(jnp.where(keep, inner, 0.0))
        syl[c] = inner
        yield
        solution_bar = mul_cat([(cl[c], grad), (kt[c], inner)])
        yield
        xb[c] = solution_bar
        search, image = pf[last, c], wf[last, c]
        alpha = al[last, c]
        ratio = colsum(solution_bar * search) * pws[last, c]
        curve_bar = -ratio * alpha
        wbl[last, c] = left(scaled(curve_bar, search))
        halves = sl[last, c]
        sbl[last, c] = left(
            scaled(curve_bar, halves[:, :CH].astype(F32) + halves[:, CH:].astype(F32))
        )
        pb[c] = scaled(alpha, solution_bar) + scaled(2.0 * curve_bar, image)
        rrb[c] = ratio
        yield
        for step in range(last - 1, -1, -1):
            search, search_bar = pf[step, c], pb[c]
            alpha, beta = al[step, c], be[step, c]
            beta_bar = colsum(search_bar * search) * ivs[step, c]
            next_bar = 2.0 * (rrb[c] + beta_bar)
            yield
            residual_bar = search_bar + scaled(next_bar, rf[step, c])
            if step + 1 < last:
                residual_bar = residual_bar + rb[c]
            rb[c] = residual_bar
            image, solution_bar = wf[step, c], xb[c]
            ratio = colsum(solution_bar * search - residual_bar * image) * pws[step, c]
            curve_bar = -ratio * alpha
            rrb[c] = ratio - beta_bar * beta
            image_bar = scaled(curve_bar, search) - scaled(alpha, residual_bar)
            halves = left(image_bar)
            wbl[step, c] = halves
            pb[c] = (
                scaled(beta, search_bar) + scaled(alpha, solution_bar)
                + scaled(curve_bar, image) + scaled(damping[c], image_bar)
            )
            yield
            both = fold(jnp.dot(ak[c], right(halves), preferred_element_type=F32))
            yield
            inner = left(jnp.where(keep, both[DH:], 0.0))
            sbl[step, c] = inner
            yield
            pb[c] = pb[c] + (both[:DH] + mul(kt[c], inner))
            yield

    interleave([backward(c) for c in range(nch)], (0,1,3,4))

    total = jnp.zeros((DH, DH), F32)
    for c in range(nch):
        part = mul_t([(pl_[j, c], wbl[j, c]) for j in range(ITERS)])
        dsy[c] = part
        total = total + part
    send_first(2, total + total.T)
    total = jnp.zeros((DH, DH), F32)
    for c in range(nch):
        part = mul_t([(xl[c], yl[c])])
        dcc[c] = part
        total = total + part
    send_first(3, total)

    for c in range(nch):
        o_normed[rows[c], :] = (mx[c] * inverse[c : c + 1, :]).T * gain_in[...]
        grad = rb[c] + pb[c] + scaled(2.0 * rrb[c], pf[0, c])
        o_gq[rows[c], :] = grad.T

    def key_part(c):
        pairs = [(syl[c], xl[c])]
        for j in range(ITERS):
            pairs.append((sl[j, c], wbl[j, c]))
            pairs.append((sbl[j, c], pl_[j, c]))
        o_gk[rows[c], :] = mul_t(pairs)

    key_part(0)
    key_part(1)
    send_second(2, True, None)
    send_second(3, True, None)
    key_part(2)
    key_part(3)
    later = jnp.zeros((DH, DH), F32)
    for c in range(nch - 1, -1, -1):
        o_gv[rows[c], :] = mul_t([(sxl[c], yl[c])])
        if c + 1 < nch:
            o_gk[rows[c], :] += mul(ak[c, DH:, :], left(later))
        later = later + (dsy[c] + dsy[c].T)

    cross = finish(3)
    for c in range(nch - 1, -1, -1):
        halves = left(cross)
        o_gv[rows[c], :] += mul(ak[c, DH:, :], halves)
        o_gk[rows[c], :] += mul_t([(vl[c], halves)])
        cross = cross + dcc[c]
    halves = left(finish(2))
    for c in range(nch):
        o_gk[rows[c], :] += mul(ak[c, DH:, :], halves)

    bytes_wait(stat_in, n_head - 1, hs.at[0])
    for x in range(4):
        bytes_wait(src.at[x], n_seq - 1, s1.at[x])
        bytes_wait(buf2.at[x], n_seq - 1, s2.at[x])


def hand_over(a, b, c, d, a_out, b_out, c_out, d_out, sem):
    pairs = ((a, a_out), (b, b_out), (c, c_out), (d, d_out))
    copies = [pltpu.make_async_copy(*pair, sem.at[at]) for at, pair in enumerate(pairs)]
    for copy in copies:
        copy.start()
    for copy in copies:
        copy.wait()


def local(n_seq, n_head, queries, keys, values, gain, ridge, prior_gram, prior_cross, cotangent):
    rows, width = queries.shape
    nch = rows // CH
    pr = DH // n_seq
    anyspace = pl.BlockSpec(memory_space=pl.ANY)
    tok = pltpu.VMEM((rows, DH), F32)
    prior = pltpu.VMEM((max(pr, 8), DH), F32)
    per_chunk = pltpu.VMEM((nch, DH, CH), F32)
    halves = pltpu.VMEM((nch, DH, 2 * CH), BF16)
    per_step = pltpu.VMEM((ITERS, nch, DH, CH), F32)
    step_halves = pltpu.VMEM((ITERS, nch, DH, 2 * CH), BF16)
    scal = pltpu.VMEM((ITERS, nch, 8, CH), F32)
    exchange = pltpu.VMEM((4, n_seq, pr, DH), F32)
    scratch = [
        tok, tok, tok, tok, prior, prior, pltpu.VMEM((1, DH), F32), pltpu.SMEM((1,), F32),
        pltpu.VMEM((nch, 2 * DH, 2 * CH), BF16), halves, halves, halves, halves, halves,
        per_chunk, per_chunk, per_chunk, per_chunk,
        per_step, per_step, per_step, step_halves, step_halves, step_halves, step_halves,
        scal, scal, scal, scal, scal,
        per_chunk, halves, per_chunk, halves, halves, halves, per_chunk, per_chunk, per_chunk,
        pltpu.VMEM((nch, 8, CH), F32), per_chunk, per_chunk,
        exchange, exchange, exchange, exchange,
        pltpu.VMEM((2 * nch, CH), F32), pltpu.VMEM((n_head, 2 * nch, CH), F32),
        pltpu.SemaphoreType.DMA((8,)),
        pltpu.SemaphoreType.DMA((4,)), pltpu.SemaphoreType.DMA((4,)),
        pltpu.SemaphoreType.DMA((4,)), pltpu.SemaphoreType.DMA((4,)),
        pltpu.SemaphoreType.DMA((1,)), pltpu.SemaphoreType.DMA((1,)),
    ]
    shape = jax.ShapeDtypeStruct((rows, width), F32)
    held = pltpu.VMEM((rows, width), F32)
    results = pl.pallas_call(
        functools.partial(kernel, n_seq, n_head, float(width * n_head)),
        out_shape=(held, held, held, held),
        in_specs=[pl.BlockSpec(memory_space=pltpu.HBM)] * 8,
        out_specs=[pl.BlockSpec(memory_space=pltpu.VMEM)] * 4,
        scratch_shapes=scratch,
        compiler_params=pltpu.CompilerParams(
            collective_id=0, has_side_effects=True, vmem_limit_bytes=65800000
        ),
    )(
        queries, keys, values, gain.reshape(1, width), ridge,
        prior_gram, prior_cross, cotangent,
    )
    return pl.pallas_call(
        hand_over,
        out_shape=(shape, shape, shape, shape),
        in_specs=[pl.BlockSpec(memory_space=pltpu.VMEM)] * 4,
        out_specs=[pl.BlockSpec(memory_space=pltpu.HBM)] * 4,
        scratch_shapes=[pltpu.SemaphoreType.DMA((4,))],
        compiler_params=pltpu.CompilerParams(vmem_limit_bytes=1024 * 1024),
    )(*results)


def solution(mesh):
    in_specs = (
        P("seq", "head"),
        P("seq", "head"),
        P("seq", "head"),
        P("head"),
        P("head"),
        P("head", None, None),
        P("head", None, None),
        P("seq", "head"),
    )
    out_specs = (P("seq", "head"), P("seq", "head"), P("seq", "head"), P("seq", "head"))
    body = functools.partial(local, mesh.shape["seq"], mesh.shape["head"])
    return jax.shard_map(body, mesh=mesh, in_specs=in_specs, out_specs=out_specs, check_vma=False)
```

time: 449 us -> 47.7 us (0.11)
  waiting for transfers between devices: 170 us -> 0 us
  matrix products: 112 us -> 0 us
  other arithmetic: 89.9 us -> 0 us
  Pallas kernels: 0 us -> 46.3 us
  local copies, waits for them, and re-layouts: 42.8 us -> 0 us
  blocking collectives: 13.8 us -> 0 us
  between operations: 14.3 us -> 1.29 us
    all_gather x4 -> x0, waiting for transfers between devices: 169 us -> none  [prefix(): gathered = jax.tree.map(lambda a: lax.all_gather(a, axis), part)]
    dot_general x111 -> x0, matrix products: 112 us -> none  [the longest x32 43.5 us: apply_system(): jnp.dot(inner, keyset, precision=highest)]
    pallas_call x0 -> x2, Pallas kernels: none -> 46.3 us  [the longest x1 45.3 us: local(): pl.pallas_call(functools.partial(kernel, n_seq, n_head, float(width * n_h...]
    add x49 -> x0, other arithmetic: 31.8 us -> none  [the longest x31 28.2 us: add_pair(): return (earlier[0] + later[0], earlier[1] + later[1])]
    dynamic_slice x56 -> x0, local copies, waits for them, and re-layouts: 30.2 us -> none  [block_forward(): (solution, _, _, _), _ = lax.scan(cg_step, start, None, length=ITERS)]
    dynamic_update_slice x32 -> x0, other arithmetic: 21.7 us -> none  [block_forward(): (solution, _, _, _), _ = lax.scan(cg_step, start, None, length=ITERS)]
    mul x25 -> x0, other arithmetic: 15.7 us -> none  [the longest x24 15.7 us: block_forward(): ridge_value * (first_row + places + 1).astype(jnp.float32)[:, None]]
    psum x1 -> x0, blocking collectives: 13.8 us -> none  [local(): total_square = lax.psum(local_square, 'head')]
  transfers between devices with their start and end apart: 4 -> 0, of which waited for: 3 -> 0; matrix products, arithmetic and copies ran while one was open for 25% -> 0% of each run, Pallas kernels for 0% -> 0%
where the time goes in v2:
time: 47.7 us; the launch traced here: 47.6 us
  Pallas kernels  46.3 us (97%)
  between operations  1.29 us (3%)
    pallas_call x1, Pallas kernels, local(): pl.pallas_call(functools.partial(kernel, n_seq, n_head, float(width * n_h...  45.3 us
    pallas_call x1, Pallas kernels, local(): pl.pallas_call(hand_over, out_shape=(shape, shape, shape, shape), in_spec...  1 us

profile of v2, /device:TPU:1, one launch (start us, length us, event | category | flops | bytes accessed | tf_op | source)
XLA Modules:
  0.0 47.6 jit_solution(14367376476814363500)
XLA Ops:
  1.3 45.3 %shard_map.111 = (f32[512,128]{1,0:T(8,128)S(1)}, f32[512,128]{1,0:T(8,128)S(1)}, f32[512,128]{1,0:T(8,128)S(1)}, f32[512,128]{1,0:T(8,128)S(1)}) custom-call(f32[512,128]{1,0:T(8,128)} %q_hbm.1, f32[512,128]{1,0:T(8,128)} %k_hbm.1, f32[512,128]{1,0:T(8,128)} %v_hbm.1, f32[1,128]{1,0:T(1,128)} %bitcast.1, f32[1]{0:T(128)S(6)} %copy.12.ridge_hbm, ...), custom_call_target="tpu_custom_call" | custom-call | tf_op jit(solution)/shard_map/pallas_call | solution.py:462
  46.6 1.0 %shard_map.112 = (f32[512,128]{1,0:T(8,128)}, f32[512,128]{1,0:T(8,128)}, f32[512,128]{1,0:T(8,128)}, f32[512,128]{1,0:T(8,128)}) custom-call(f32[512,128]{1,0:T(8,128)S(1)} %get-tuple-element.8.a, f32[512,128]{1,0:T(8,128)S(1)} %get-tuple-element.9.b, f32[512,128]{1,0:T(8,128)S(1)} %get-tuple-element.10.c, f32[512,128]{1,0:T(8,128)S(1)} %get-tuple-element.11.d), custom_call_target="tpu_custom_call" | custom-call | tf_op jit(solution)/shard_map/pallas_call | solution.py:475

commit v3 on v2

--- a/solution.py
+++ b/solution.py
@@ -93,7 +93,7 @@
     q_in, k_in, v_in, cot_in, pg_in, pc_in, gain_in, ridge_in,
     ak, kt, vl, vtl, cl, ctl, mg, mc, qt, ct,
     pf, wf, rf, pl_, sl, wbl, sbl, al, be, rrs, pws, ivs,
-    xt, xl, mx, sxl, syl, yl, xb, pb, rb, rrb, dsy, dcc,
+    xt, xl, mx, sxl, syl, yl, xb, xm, ml, pb, rb, rrb, dsy, dcc,
     src, recv1, buf2, recv2, stat, stat_in,
     in_sem, s1, r1, s2, r2, hs, hr,
 ):
@@ -115,22 +115,6 @@
         loads.append(copy)
 
     barrier = pltpu.get_barrier_semaphore()
-
-    def greet_seq(turn, carry):
-        pl.semaphore_signal(
-            barrier, inc=1, device_id={"seq": lax.rem(me + turn, n_seq)}, device_id_type=MESH
-        )
-        return carry
-
-    def greet_head(turn, carry):
-        pl.semaphore_signal(
-            barrier, inc=1, device_id={"head": lax.rem(my_head + turn, n_head)},
-            device_id_type=MESH,
-        )
-        return carry
-
-    lax.fori_loop(1, n_seq, greet_seq, 0)
-    lax.fori_loop(1, n_head, greet_head, 0)
 
     if n_seq == 32:
         offsets = [(x, y, z) for x in range(4) for y in range(4) for z in range(2)]
@@ -144,6 +128,13 @@
     else:
         others = [lax.rem(me + turn, n_seq) for turn in range(1, n_seq)]
     turns = sorted(range(1, n_head), key=lambda turn: -min(turn, n_head - turn))
+    for device in others:
+        pl.semaphore_signal(barrier, inc=1, device_id={"seq": device}, device_id_type=MESH)
+    for turn in turns:
+        pl.semaphore_signal(
+            barrier, inc=1, device_id={"head": lax.rem(my_head + turn, n_head)},
+            device_id_type=MESH,
+        )
 
     def bytes_wait(ref, count, sem):
         view = ref.at[pl.ds(0, count)]
@@ -216,6 +207,7 @@
         pl_[0, c] = left(start)
         rrs[0, c] = colsum(start * start)
         xt[c] = jnp.zeros_like(start)
+        sl[0, c] = left(jnp.where(keep, mul(ak[c, DH:, :], pl_[0, c]), 0.0))
     for c in range(nch - 1):
         mg[c] = mul(kt[c], ak[c, DH:, :])
     loads[3].wait()
@@ -238,12 +230,16 @@
 
     def forward(c):
         for step in range(ITERS):
-            both = fold(jnp.dot(ak[c], right(pl_[step, c]), preferred_element_type=F32))
-            yield
-            inner = left(jnp.where(keep, both[DH:], 0.0))
-            sl[step, c] = inner
-            yield
-            image = both[:DH] + mul(kt[c], inner)
+            halves = pl_[step, c]
+            if step == 0:
+                inner = sl[0, c]
+            else:
+                inner = mul(ak[c, DH:, :], halves)
+                yield
+                inner = left(jnp.where(keep, inner, 0.0))
+                sl[step, c] = inner
+                yield
+            image = mul_cat([(ak[c, :DH, :], halves), (kt[c], inner)])
             yield
             search = pf[step, c]
             image = image + scaled(damping[c], search)
@@ -272,14 +268,22 @@
                 xl[c] = left(xt[c])
             yield
 
-    interleave([forward(c) for c in range(nch)], (0,1,3,4))
-
-    cross = finish(1)
-    for c in range(nch):
-        ctl[c] = left(cross.T)
-        cl[c] = left(cross)
-        if c + 1 < nch:
-            cross = cross + mc[c]
+    def cross_states():
+        cross = finish(1)
+        for c in range(nch):
+            yield
+            ctl[c] = left(cross.T)
+            cl[c] = left(cross)
+            if c + 1 < nch:
+                cross = cross + mc[c]
+            yield
+            grad = left(ct[c])
+            inner = left(jnp.where(keep, mul(vl[c], grad), 0.0))
+            yield
+            xb[c] = mul_cat([(cl[c], grad), (kt[c], inner)])
+            yield
+
+    interleave([forward(c) for c in range(nch)] + [cross_states()], (0, 0, 0, 0, 12))
 
     def read_out(c):
         inner = mul(ak[c, DH:, :], xl[c])
@@ -302,6 +306,10 @@
             device_id={"head": lax.rem(my_head + turn, n_head)}, device_id_type=MESH,
         ).start()
     stat_in[my_head] = stat[...]
+    for c in range(nch):
+        ml[c] = left(mx[c])
+        inner = left(jnp.where(keep, mul(vl[c], ml[c]), 0.0))
+        xm[c] = mul_cat([(cl[c], ml[c]), (kt[c], inner)])
     bytes_wait(stat_in, n_head - 1, hr.at[0])
     sums = stat_in[0]
     for device in range(1, n_head):
@@ -311,16 +319,18 @@
 
     last = ITERS - 1
 
+    def push_back(c, step, halves):
+        inner = mul(ak[c, DH:, :], halves)
+        yield
+        inner = left(jnp.where(keep, inner, 0.0))
+        sbl[step, c] = inner
+        yield
+        pb[c] = pb[c] + mul_cat([(ak[c, :DH, :], halves), (kt[c], inner)])
+
     def backward(c):
-        grad = left(inverse[c : c + 1, :] * ct[c] - mx[c] * pull[c : c + 1, :])
-        yl[c] = grad
-        inner = mul(vl[c], grad)
-        yield
-        inner = left(jnp.where(keep, inner, 0.0))
-        syl[c] = inner
-        yield
-        solution_bar = mul_cat([(cl[c], grad), (kt[c], inner)])
-        yield
+        keep_part = jnp.broadcast_to(inverse[c : c + 1, :], (8, CH))
+        norm_part = jnp.broadcast_to(pull[c : c + 1, :], (8, CH))
+        solution_bar = scaled(keep_part, xb[c]) - scaled(norm_part, xm[c])
         xb[c] = solution_bar
         search, image = pf[last, c], wf[last, c]
         alpha = al[last, c]
@@ -356,30 +366,33 @@
                 + scaled(curve_bar, image) + scaled(damping[c], image_bar)
             )
             yield
-            both = fold(jnp.dot(ak[c], right(halves), preferred_element_type=F32))
-            yield
-            inner = left(jnp.where(keep, both[DH:], 0.0))
-            sbl[step, c] = inner
-            yield
-            pb[c] = pb[c] + (both[:DH] + mul(kt[c], inner))
-            yield
-
-    interleave([backward(c) for c in range(nch)], (0,1,3,4))
-
-    total = jnp.zeros((DH, DH), F32)
-    for c in range(nch):
-        part = mul_t([(pl_[j, c], wbl[j, c]) for j in range(ITERS)])
-        dsy[c] = part
-        total = total + part
+            if step % 2 == 0:
+                part = mul_t([(pl_[j, c], wbl[j, c]) for j in (step + 1, step)])
+                dsy[c] = part if step + 2 > last else dsy[c] + part
+            if step > 0:
+                yield from push_back(c, step, halves)
+                yield
+
+    def cross_back():
+        total = jnp.zeros((DH, DH), F32)
+        for c in range(nch):
+            yl[c] = left(inverse[c : c + 1, :] * ct[c] - mx[c] * pull[c : c + 1, :])
+            part = mul_t([(xl[c], yl[c])])
+            dcc[c] = part
+            total = total + part
+            yield
+        send_first(3, total)
+        yield
+
+    interleave([backward(c) for c in range(nch)] + [cross_back()], (0, 0, 0, 0, 2))
+
+    total = dsy[0]
+    for c in range(1, nch):
+        total = total + dsy[c]
     send_first(2, total + total.T)
-    total = jnp.zeros((DH, DH), F32)
-    for c in range(nch):
-        part = mul_t([(xl[c], yl[c])])
-        dcc[c] = part
-        total = total + part
-    send_first(3, total)
-
-    for c in range(nch):
+    interleave([push_back(c, 0, wbl[0, c]) for c in range(nch)], (0, 0, 0, 0))
+    for c in range(nch):
+        syl[c] = left(jnp.where(keep, mul(vl[c], yl[c]), 0.0))
         o_normed[rows[c], :] = (mx[c] * inverse[c : c + 1, :]).T * gain_in[...]
         grad = rb[c] + pb[c] + scaled(2.0 * rrb[c], pf[0, c])
         o_gq[rows[c], :] = grad.T
@@ -391,10 +404,10 @@
             pairs.append((sbl[j, c], pl_[j, c]))
         o_gk[rows[c], :] = mul_t(pairs)
 
+    send_second(3, True, None)
     key_part(0)
+    send_second(2, True, None)
     key_part(1)
-    send_second(2, True, None)
-    send_second(3, True, None)
     key_part(2)
     key_part(3)
     later = jnp.zeros((DH, DH), F32)
@@ -448,7 +461,7 @@
         per_chunk, per_chunk, per_chunk, per_chunk,
         per_step, per_step, per_step, step_halves, step_halves, step_halves, step_halves,
         scal, scal, scal, scal, scal,
-        per_chunk, halves, per_chunk, halves, halves, halves, per_chunk, per_chunk, per_chunk,
+        per_chunk, halves, per_chunk, halves, halves, halves, per_chunk, per_chunk, halves, per_chunk, per_chunk,
         pltpu.VMEM((nch, 8, CH), F32), per_chunk, per_chunk,
         exchange, exchange, exchange, exchange,
         pltpu.VMEM((2 * nch, CH), F32), pltpu.VMEM((n_head, 2 * nch, CH), F32),

time: 47.7 us -> 46.1 us (0.966)
  Pallas kernels: 46.3 us -> 44.7 us
    pallas_call x1, Pallas kernels: 45.3 us -> 43.7 us  [local(): pl.pallas_call(functools.partial(kernel, n_seq, n_head, float(width * n_h...]
where the time goes in v3:
time: 46.1 us; the launch traced here: 46 us
  Pallas kernels  44.7 us (97%)
  between operations  1.29 us (3%)
    pallas_call x1, Pallas kernels, local(): pl.pallas_call(functools.partial(kernel, n_seq, n_head, float(width * n_h...  43.7 us
    pallas_call x1, Pallas kernels, local(): pl.pallas_call(hand_over, out_shape=(shape, shape, shape, shape), in_spec...  1 us

profile of v3, /device:TPU:1, one launch (start us, length us, event | category | flops | bytes accessed | tf_op | source)
XLA Modules:
  0.0 46.0 jit_solution(4141417343527783087)
XLA Ops:
  1.3 43.7 %shard_map.111 = (f32[512,128]{1,0:T(8,128)S(1)}, f32[512,128]{1,0:T(8,128)S(1)}, f32[512,128]{1,0:T(8,128)S(1)}, f32[512,128]{1,0:T(8,128)S(1)}) custom-call(f32[512,128]{1,0:T(8,128)} %q_hbm.1, f32[512,128]{1,0:T(8,128)} %k_hbm.1, f32[512,128]{1,0:T(8,128)} %v_hbm.1, f32[1,128]{1,0:T(1,128)} %bitcast.1, f32[1]{0:T(128)S(6)} %copy.12.ridge_hbm, ...), custom_call_target="tpu_custom_call" | custom-call | tf_op jit(solution)/shard_map/pallas_call | solution.py:475
  45.0 1.0 %shard_map.112 = (f32[512,128]{1,0:T(8,128)}, f32[512,128]{1,0:T(8,128)}, f32[512,128]{1,0:T(8,128)}, f32[512,128]{1,0:T(8,128)}) custom-call(f32[512,128]{1,0:T(8,128)S(1)} %get-tuple-element.8.a, f32[512,128]{1,0:T(8,128)S(1)} %get-tuple-element.9.b, f32[512,128]{1,0:T(8,128)S(1)} %get-tuple-element.10.c, f32[512,128]{1,0:T(8,128)S(1)} %get-tuple-element.11.d), custom_call_target="tpu_custom_call" | custom-call | tf_op jit(solution)/shard_map/pallas_call | solution.py:488

commit v4 on v3

--- a/solution.py
+++ b/solution.py
@@ -424,8 +424,7 @@
         o_gk[rows[c], :] += mul_t([(vl[c], halves)])
         cross = cross + dcc[c]
     halves = left(finish(2))
-    for c in range(nch):
-        o_gk[rows[c], :] += mul(ak[c, DH:, :], halves)
+    o_gk[...] += mul(jnp.concatenate([ak[c, DH:, :] for c in range(nch)], axis=0), halves)
 
     bytes_wait(stat_in, n_head - 1, hs.at[0])
     for x in range(4):

time: 46.1 us -> 46.1 us (level)
  no operation moved by 1% of the time
where the time goes in v4:
time: 46.1 us; the launch traced here: 46 us
  Pallas kernels  44.7 us (97%)
  between operations  1.29 us (3%)
    pallas_call x1, Pallas kernels, local(): pl.pallas_call(functools.partial(kernel, n_seq, n_head, float(width * n_h...  43.7 us
    pallas_call x1, Pallas kernels, local(): pl.pallas_call(hand_over, out_shape=(shape, shape, shape, shape), in_spec...  1 us

profile of v4, /device:TPU:1, one launch (start us, length us, event | category | flops | bytes accessed | tf_op | source)
XLA Modules:
  0.0 46.0 jit_solution(11370398591921784782)
XLA Ops:
  1.3 43.7 %shard_map.111 = (f32[512,128]{1,0:T(8,128)S(1)}, f32[512,128]{1,0:T(8,128)S(1)}, f32[512,128]{1,0:T(8,128)S(1)}, f32[512,128]{1,0:T(8,128)S(1)}) custom-call(f32[512,128]{1,0:T(8,128)} %q_hbm.1, f32[512,128]{1,0:T(8,128)} %k_hbm.1, f32[512,128]{1,0:T(8,128)} %v_hbm.1, f32[1,128]{1,0:T(1,128)} %bitcast.1, f32[1]{0:T(128)S(6)} %copy.12.ridge_hbm, ...), custom_call_target="tpu_custom_call" | custom-call | tf_op jit(solution)/shard_map/pallas_call | solution.py:474
  45.0 1.0 %shard_map.112 = (f32[512,128]{1,0:T(8,128)}, f32[512,128]{1,0:T(8,128)}, f32[512,128]{1,0:T(8,128)}, f32[512,128]{1,0:T(8,128)}) custom-call(f32[512,128]{1,0:T(8,128)S(1)} %get-tuple-element.8.a, f32[512,128]{1,0:T(8,128)S(1)} %get-tuple-element.9.b, f32[512,128]{1,0:T(8,128)S(1)} %get-tuple-element.10.c, f32[512,128]{1,0:T(8,128)S(1)} %get-tuple-element.11.d), custom_call_target="tpu_custom_call" | custom-call | tf_op jit(solution)/shard_map/pallas_call | solution.py:487
